TPU v7x, 128 devices: a whole 4x4x4 slice. The times are simulated.
128 devices in a mesh: prow: 8 (over z, core), pcol: 16 (over x, y).
Axes of the slice: x: 4, y: 4, z: 4, core: 2. Of those that a mesh axis runs over, the one named last changes fastest.
Arguments:
- factors: bfloat16 [4, 4096, 512], P(None, ('prow', 'pcol')), may hold values from -0.25 to 0.25
- x_factor: bfloat16 [512, 512], replicated, may hold values from -0.25 to 0.25
- zinv_factor: bfloat16 [512, 512], replicated, may hold values from -0.25 to 0.25
- placement: int32 [4096], replicated, may hold values from 0 to 4095, as said below
Outputs:
- trailing: float32 [4096, 4096], P('prow', 'pcol')
- panels: float32 [4096, 1024], P('prow', 'pcol')
Inputs may be any that keep to these rules, and one draw needn't show every extreme that they name: placement is a permutation of the Schur rows; device d (grid rows slowest) assembles the rows placement[d * 32] to placement[d * 32 + 31]; among one device's rows at most 8 share the same owner grid row (natural row i belongs to grid row (i div 64) mod 8), and some device has exactly 8 such rows.
All inputs are finite; a program needn't handle non-finite values.
Results may differ from a plain program's by a relative error of at most 0.003.
Values may be sent and summed in bfloat16 or wider, within the bound.
A program may use at most 128 MiB of HBM per device.

v0:
```python
import jax
import jax.numpy as jnp
from jax import lax
from jax.sharding import PartitionSpec as P

RANK = 4
NB = 64
K = 1024
rank_signs = (1.0, 1.0, -1.0, -1.0)


def project(segment, factor_mat):
    span_cols = segment.shape[1]
    flat_rows = segment.reshape(RANK * span_cols, segment.shape[2])
    images = jnp.dot(flat_rows, factor_mat, preferred_element_type=jnp.float32).astype(jnp.bfloat16)
    return images.reshape(RANK, span_cols, factor_mat.shape[1])


def pair_terms(left_x, left_z, right_x, right_z):
    weights = jnp.array(rank_signs, jnp.float32)
    contract = (((1,), (1,)), ((), ()))
    span_rows = left_x.shape[1]
    span_cols = right_x.shape[1]
    width = left_x.shape[2]
    inner_x = lax.dot_general(
        left_x.reshape(RANK * span_rows, width),
        right_x.reshape(RANK * span_cols, width),
        contract,
        preferred_element_type=jnp.float32,
    )
    inner_z = lax.dot_general(
        left_z.reshape(RANK * span_rows, width),
        right_z.reshape(RANK * span_cols, width),
        contract,
        preferred_element_type=jnp.float32,
    )
    product = (inner_x * inner_z).reshape(RANK, span_rows, RANK, span_cols)
    return jnp.einsum("r,riqj,q->ij", weights, product, weights)


def per_device(factors, x_factor, zinv_factor, placement):
    prow_count = lax.axis_size("prow")
    pcol_count = lax.axis_size("pcol")
    devices_all = prow_count * pcol_count
    rows_dev = factors.shape[1]
    total_rows = placement.shape[0]
    local_rows = total_rows // prow_count
    local_cols = total_rows // pcol_count
    prow_id = lax.axis_index("prow")
    pcol_id = lax.axis_index("pcol")
    inverse = (
        jnp.zeros((total_rows,), jnp.int32)
        .at[placement]
        .set(jnp.arange(total_rows, dtype=jnp.int32))
    )
    slot_k = jnp.arange(local_rows)
    natural_k = slot_k // NB * NB * prow_count + prow_id * NB + slot_k % NB
    own_x = project(factors, x_factor)
    own_z = project(factors, zinv_factor)
    blank_rows = jnp.zeros((rows_dev, total_rows), jnp.float32)
    schur_rows = blank_rows.at[:, placement].set(
        pair_terms(
            own_x,
            own_z,
            lax.all_gather(own_x, ("prow", "pcol"), axis=1, tiled=True),
            lax.all_gather(own_z, ("prow", "pcol"), axis=1, tiled=True),
        )
    )
    device_id = lax.axis_index(("prow", "pcol"))
    my_rows = lax.dynamic_slice_in_dim(placement, device_id * rows_dev, rows_dev)
    capacity = 2 * rows_dev // prow_count
    target = my_rows // NB % prow_count
    prow_ids = jnp.arange(prow_count)
    onehot = (target[:, None] == prow_ids[None, :]).astype(jnp.int32)
    rank_in = jnp.sum((jnp.cumsum(onehot, axis=0) - onehot) * onehot, axis=1)
    select = (
        (target[None, None, :] == prow_ids[:, None, None])
        & (rank_in[None, None, :] == jnp.arange(capacity)[None, :, None])
    ).astype(jnp.float32)
    packed = jnp.dot(
        select.reshape(prow_count * capacity, rows_dev), schur_rows, precision=lax.Precision.HIGHEST
    )
    packed = packed.reshape(prow_count, capacity, total_rows // (NB * pcol_count), pcol_count, NB)
    packed = packed.transpose(0, 3, 1, 2, 4).reshape(prow_count, pcol_count, capacity, local_cols)
    received = lax.all_to_all(
        packed.reshape(devices_all, capacity, local_cols),
        ("prow", "pcol"),
        split_axis=0,
        concat_axis=0,
        tiled=True,
    )
    received = received.reshape(devices_all * capacity, local_cols)
    all_target = (placement // NB % prow_count).reshape(devices_all, rows_dev)
    earlier = jnp.arange(rows_dev)[None, :, None] > jnp.arange(rows_dev)[None, None, :]
    slot_ranks = jnp.sum(
        ((all_target[:, :, None] == all_target[:, None, :]) & earlier).astype(jnp.int32), axis=2
    ).reshape(total_rows)
    position = inverse[natural_k]
    flat_index = position // rows_dev * capacity + slot_ranks[position]
    schur_local = received[flat_index]
    lead_cols = K // pcol_count
    front_cols = schur_local[:, :lead_cols]
    row_panel = lax.all_gather(front_cols, "pcol", axis=1, tiled=True)
    row_panel = (
        row_panel.reshape(local_rows, pcol_count, lead_cols // NB, NB)
        .transpose(0, 2, 1, 3)
        .reshape(local_rows, K)
    )
    lead_rows = K // prow_count
    top_panel, top_cols = (
        lax.all_gather(row_panel[:lead_rows], "prow", axis=0, tiled=True),
        lax.all_gather(schur_local[:lead_rows], "prow", axis=0, tiled=True),
    )

    def natural_rows(stacked):
        return (
            stacked.reshape(prow_count, lead_rows // NB, NB, stacked.shape[1])
            .transpose(1, 0, 2, 3)
            .reshape(K, stacked.shape[1])
        )

    leading = jnp.linalg.cholesky(natural_rows(top_panel))
    panel_rows = lax.linalg.triangular_solve(
        leading, row_panel, left_side=False, lower=True, transpose_a=True
    )
    panel_cols = lax.linalg.triangular_solve(
        leading, natural_rows(top_cols).T, left_side=False, lower=True, transpose_a=True
    )
    trailing = schur_local - jnp.dot(panel_rows, panel_cols.T, precision=lax.Precision.HIGHEST)
    own_panel = lax.dynamic_index_in_dim(
        panel_rows.reshape(local_rows, K // (NB * pcol_count), pcol_count, NB),
        pcol_id,
        2,
        keepdims=False,
    )
    return (trailing, own_panel.reshape(local_rows, K // pcol_count))


def solution(mesh):
    in_specs = (P(None, ("prow", "pcol"), None), P(), P(), P())
    out_specs = (P("prow", "pcol"), P("prow", "pcol"))
    return jax.shard_map(
        per_device, mesh=mesh, in_specs=in_specs, out_specs=out_specs, check_vma=False
    )
```

profile of v0, /device:TPU:1, one launch (start us, length us, event | category | flops | bytes accessed | tf_op | source)
XLA Modules:
  0.0 744.0 jit_solution(3466437488755991065)
XLA Ops:
  14.9 80.7 %all-gather.6.cloned.1.call-done = bf16[4,4096,512]{2,1,0:T(8,128)(2,1)} async-done(((bf16[4,32,512]{2,1,0:T(8,128)(2,1)}), bf16[4,4096,512]{2,1,0:T(8,128)(2,1)}) %all-gather.6.cloned.1.call-update) | async-done | bytes 16777232 | tf_op jit(solution)/shard_map/all_gather | solution.py:65
  95.5 14.6 %fusion.113 = f32[128,16384]{1,0:T(8,128)} fusion(bf16[128,512]{1,0:T(8,128)(2,1)} %convolution_convert_fusion.1, bf16[16384,512]{1,0:T(8,128)(2,1)} %bitcast.189), kind=kOutput, calls=%fused_computation.289 | convolution fusion | flops 2147483648 | bytes 25296896 | tf_op jit(solution)/shard_map/dot_general | solution.py:25
  110.1 68.9 %all-gather.8.cloned.1.call-done = bf16[4,4096,512]{2,1,0:T(8,128)(2,1)} async-done(((bf16[4,32,512]{2,1,0:T(8,128)(2,1)}), bf16[4,4096,512]{2,1,0:T(8,128)(2,1)}) %all-gather.8.cloned.1.call-update) | async-done | bytes 16777232 | tf_op jit(solution)/shard_map/all_gather | solution.py:66
  179.0 12.9 %convolution_multiply_fusion = f32[128,16384]{1,0:T(8,128)} fusion(f32[128,16384]{1,0:T(8,128)} %fusion.113, bf16[128,512]{1,0:T(8,128)(2,1)S(1)} %copy-done.4, bf16[16384,512]{1,0:T(8,128)(2,1)} %bitcast.187), kind=kOutput, calls=%fused_computation.7 | convolution fusion | flops 2149580800 | bytes 33685504 | tf_op jit(solution)/shard_map/dot_general | solution.py:31
  191.9 10.8 %reshape.351 = f32[4,32,4,4096]{3,2,1,0:T(4,128)} reshape(f32[128,16384]{1,0:T(8,128)} %convolution_multiply_fusion) | data formatting | bytes 16777216 | tf_op jit(solution)/shard_map/reshape | solution.py:37
  202.7 6.4 multiply_reduce_fusion
  209.8 12.5 %scatter_custom_fusion = f32[32,4096]{0,1:T(8,128)} fusion(s32[4096]{0:T(1024)S(1)} %get-tuple-element.100, f32[32,4096]{0,1:T(8,128)S(1)} %copy.66, f32[]{:T(128)} %constant.382.clone.1), kind=kCustom, calls=%fused_computation.13 | custom fusion | bytes 2621444 | tf_op jit(solution)/shard_map/scatter | solution.py:61
  222.3 4.7 convolution_bitcast_fusion
  230.5 7.4 all-to-all-start
  238.0 15.5 %scatter_custom_fusion.1 = s32[4096]{0:T(1024)S(1)} fusion(s32[4096]{0:T(1024)S(1)} %get-tuple-element.100, s32[4096]{0:T(1024)S(1)} %iota.176, s32[]{:T(128)} %copy.145), kind=kCustom, calls=%fused_computation.235 | custom fusion | bytes 16388 | tf_op jit(solution)/shard_map/scatter | solution.py:54
  254.1 3.1 gather_fusion
  257.3 3.1 gather_fusion.1
  263.7 44.1 %all-gather.10.cloned.1.call-done = f32[512,1024]{0,1:T(8,128)} async-done(((f32[512,64]{0,1:T(8,128)}), f32[512,1024]{0,1:T(8,128)}) %all-gather.10.cloned.1.call-update) | async-done | bytes 2097168 | tf_op jit(solution)/shard_map/all_gather | solution.py:103
  309.9 24.3 %all-gather.14.cloned.1.call-done = f32[1024,256]{1,0:T(8,128)} async-done(((f32[128,256]{1,0:T(8,128)}), f32[1024,256]{1,0:T(8,128)}) %all-gather.14.cloned.1.call-update) | async-done | bytes 1048592 | tf_op jit(solution)/shard_map/all_gather | solution.py:112
  341.1 27.4 %all-gather.12.cloned.1.call-done = f32[1024,1024]{1,0:T(8,128)} async-done(((f32[128,1024]{1,0:T(8,128)}), f32[1024,1024]{1,0:T(8,128)}) %all-gather.12.cloned.1.call-update) | async-done | bytes 4194320 | tf_op jit(solution)/shard_map/all_gather | solution.py:111
  368.5 4.7 copy.50
  373.2 5.5 copy.51
  378.7 4.4 fusion
  385.1 11.7 %cholesky.223 = f32[128,128]{1,0:T(8,128)S(1)} custom-call(f32[128,128]{1,0:T(8,128)S(1)} %cholesky.580), custom_call_target="Cholesky" | custom-call | tf_op jit(solution)/shard_map/jit(cholesky)/cholesky | solution.py:122
  396.8 2.5 cholesky.255
  399.4 9.8 %custom-call.64 = f32[1,128,128]{1,2,0:T(8,128)S(1)} custom-call(f32[1,128,128]{2,1,0:T(8,128)S(1)} %get-tuple-element.98), custom_call_target="InvertDiagBlocksLowerTriangular" | custom-call | tf_op jit(solution)/shard_map/jit(cholesky)/cholesky | solution.py:122
  413.1 11.9 %cholesky.244 = f32[128,128]{1,0:T(8,128)S(1)} custom-call(f32[128,128]{1,0:T(8,128)S(1)} %cholesky.584), custom_call_target="Cholesky" | custom-call | tf_op jit(solution)/shard_map/jit(cholesky)/cholesky | solution.py:122
  426.9 9.8 %custom-call.65 = f32[1,128,128]{1,2,0:T(8,128)S(1)} custom-call(f32[1,128,128]{2,1,0:T(8,128)S(1)} %get-tuple-element.95), custom_call_target="InvertDiagBlocksLowerTriangular" | custom-call | tf_op jit(solution)/shard_map/jit(cholesky)/cholesky | solution.py:122
  440.1 11.7 %cholesky.468 = f32[128,128]{1,0:T(8,128)S(1)} custom-call(f32[128,128]{1,0:T(8,128)S(1)} %cholesky.589), custom_call_target="Cholesky" | custom-call | tf_op jit(solution)/shard_map/jit(cholesky)/cholesky | solution.py:122
  453.2 9.8 %custom-call.66 = f32[1,128,128]{1,2,0:T(8,128)S(1)} custom-call(f32[1,128,128]{2,1,0:T(8,128)S(1)} %get-tuple-element.92), custom_call_target="InvertDiagBlocksLowerTriangular" | custom-call | tf_op jit(solution)/shard_map/jit(cholesky)/cholesky | solution.py:122
  466.5 12.1 %cholesky.487 = f32[128,128]{1,0:T(8,128)S(1)} custom-call(f32[128,128]{1,0:T(8,128)S(1)} %cholesky.594), custom_call_target="Cholesky" | custom-call | tf_op jit(solution)/shard_map/jit(cholesky)/cholesky | solution.py:122
  479.9 9.8 %custom-call.67 = f32[1,128,128]{1,2,0:T(8,128)S(1)} custom-call(f32[1,128,128]{2,1,0:T(8,128)S(1)} %get-tuple-element.89), custom_call_target="InvertDiagBlocksLowerTriangular" | custom-call | tf_op jit(solution)/shard_map/jit(cholesky)/cholesky | solution.py:122
  493.2 11.7 %cholesky.506 = f32[128,128]{1,0:T(8,128)S(1)} custom-call(f32[128,128]{1,0:T(8,128)S(1)} %cholesky.599), custom_call_target="Cholesky" | custom-call | tf_op jit(solution)/shard_map/jit(cholesky)/cholesky | solution.py:122
  506.3 9.9 %custom-call.68 = f32[1,128,128]{1,2,0:T(8,128)S(1)} custom-call(f32[1,128,128]{2,1,0:T(8,128)S(1)} %get-tuple-element.86), custom_call_target="InvertDiagBlocksLowerTriangular" | custom-call | tf_op jit(solution)/shard_map/jit(cholesky)/cholesky | solution.py:122
  519.6 11.7 %cholesky.526 = f32[128,128]{1,0:T(8,128)S(1)} custom-call(f32[128,128]{1,0:T(8,128)S(1)} %cholesky.604), custom_call_target="Cholesky" | custom-call | tf_op jit(solution)/shard_map/jit(cholesky)/cholesky | solution.py:122
  532.6 9.8 %custom-call.69 = f32[1,128,128]{1,2,0:T(8,128)S(1)} custom-call(f32[1,128,128]{2,1,0:T(8,128)S(1)} %get-tuple-element.83), custom_call_target="InvertDiagBlocksLowerTriangular" | custom-call | tf_op jit(solution)/shard_map/jit(cholesky)/cholesky | solution.py:122
  545.4 11.9 %cholesky.546 = f32[128,128]{1,0:T(8,128)S(1)} custom-call(f32[128,128]{1,0:T(8,128)S(1)} %cholesky.609), custom_call_target="Cholesky" | custom-call | tf_op jit(solution)/shard_map/jit(cholesky)/cholesky | solution.py:122
  558.5 9.8 %custom-call.70 = f32[1,128,128]{1,2,0:T(8,128)S(1)} custom-call(f32[1,128,128]{2,1,0:T(8,128)S(1)} %get-tuple-element.80), custom_call_target="InvertDiagBlocksLowerTriangular" | custom-call | tf_op jit(solution)/shard_map/jit(cholesky)/cholesky | solution.py:122
  571.0 11.7 %cholesky.564 = f32[128,128]{1,0:T(8,128)S(1)} custom-call(f32[128,128]{1,0:T(8,128)S(1)} %convolution_subtract_fusion.21), custom_call_target="Cholesky" | custom-call | tf_op jit(solution)/shard_map/jit(cholesky)/cholesky | solution.py:122
  589.2 4.8 select_select_fusion
  594.0 28.0 %while.1 = (s32[]{:T(128)}, f32[1024,1024]{1,0:T(8,128)}, s32[8,2]{0,1:T(2,128)S(1)}, f32[8,128,128]{2,1,0:T(8,128)}, s32[]{:T(128)}) while((s32[]{:T(128)}, f32[1024,1024]{1,0:T(8,128)}, s32[8,2]{0,1:T(2,128)S(1)}, f32[8,128,128]{2,1,0:T(8,128)}, s32[]{:T(128)}) %tuple.90), condition=%wide.while_cond, body=%wide.while_body.sunk | while | flops 2 | bytes 132705 | solution.py:123
  594.6 2.9 bitcast_dynamic-update-slice_fusion.2
  598.1 2.9 bitcast_dynamic-update-slice_fusion.2
  601.6 2.9 bitcast_dynamic-update-slice_fusion.2
  605.1 2.9 bitcast_dynamic-update-slice_fusion.2
  608.6 2.9 bitcast_dynamic-update-slice_fusion.2
  612.1 2.9 bitcast_dynamic-update-slice_fusion.2
  615.6 2.9 bitcast_dynamic-update-slice_fusion.2
  619.2 2.8 bitcast_dynamic-update-slice_fusion.2
  622.0 79.8 %custom-call.71 = f32[8,128,128]{1,2,0:T(8,128)S(1)} custom-call(f32[8,128,128]{2,1,0:T(8,128)} %get-tuple-element.9), custom_call_target="InvertDiagBlocksLowerTriangular" | custom-call | tf_op jit(solution)/shard_map/triangular_solve | solution.py:123
  725.6 2.6 convolution_subtract_fusion.8
  728.7 3.1 convolution_subtract_fusion.4
  732.2 4.4 convolution_subtract_fusion
  (156 shorter events, 89.4 us)
Async XLA Ops:
  7.2 1.1 copy-start
  7.2 88.4 %all-gather.6.cloned.1.call-start = ((), (), s32[]{:S(2)}) async-start(), calls=%async_computation.1 | async-start | bytes 16908288 | tf_op jit(solution)/shard_map/all_gather | solution.py:65
  10.0 168.9 %all-gather.8.cloned.1.call-start = ((), (), s32[]{:S(2)}) async-start(), calls=%async_computation.2 | async-start | bytes 16908288 | tf_op jit(solution)/shard_map/all_gather | solution.py:66
  95.5 83.4 %copy-start.4 = (bf16[128,512]{1,0:T(8,128)(2,1)S(1)}, bf16[128,512]{1,0:T(8,128)(2,1)}, u32[]{:S(2)}) copy-start(bf16[128,512]{1,0:T(8,128)(2,1)} %convolution_convert_fusion) | copy-start | bytes 393220
  230.5 30.0 %all-to-all-start = ((f32[128,8,256]{2,1,0:T(8,128)}), f32[128,8,256]{2,1,0:T(8,128)S(1)}, u32[]{:S(2)}, u32[]{:S(2)}) async-start(f32[128,8,256]{2,1,0:T(8,128)} %reshape_reshape.3), calls=%async_computation | async-start | bytes 2097152 | tf_op jit(solution)/shard_map/all_to_all | solution.py:85
  237.9 69.8 %all-gather.10.cloned.1.call-start = ((), (), s32[]{:S(2)}) async-start(), calls=%async_computation.3 | async-start | bytes 2228224 | tf_op jit(solution)/shard_map/all_gather | solution.py:103
  262.9 71.2 %all-gather.14.cloned.1.call-start = ((), (), s32[]{:S(2)}) async-start(), calls=%async_computation.5 | async-start | bytes 1179648 | tf_op jit(solution)/shard_map/all_gather | solution.py:112
  263.6 104.9 %all-gather.12.cloned.1.call-start = ((), (), s32[]{:S(2)}) async-start(), calls=%async_computation.4 | async-start | bytes 4718592 | tf_op jit(solution)/shard_map/all_gather | solution.py:111
  383.2 1.9 copy-start.3
  701.8 6.0 copy-start.2
  708.8 7.1 copy-start.5
  710.4 6.6 copy-start.6
  716.0 4.7 copy-start.8
  722.5 6.2 copy-start.7
  728.2 9.0 %copy-start.1 = (bf16[512,512]{1,0:T(8,128)(2,1)S(1)}, bf16[512,512]{1,0:T(8,128)(2,1)}, u32[]{:S(2)}) copy-start(bf16[512,512]{1,0:T(8,128)(2,1)} %param.6) | copy-start | bytes 1572868
Sparse Core Ops, SparseCore 0:
  11.6 83.9 all-gather.5
  99.1 79.8 all-gather.7
  263.0 44.6 all-gather.9
  309.3 24.7 all-gather.13
  336.3 32.1 all-gather.11
where the time goes:
time: 754 us; the launch traced here: 744 us
  other arithmetic  272 us (36%)
  waiting for transfers between devices  245 us (32%)
  local copies, waits for them, and re-layouts  106 us (14%)
  matrix products  93.6 us (12%)
  between operations  19.9 us (3%)
  starting transfers between devices  7.58 us (1%)
    another operation x31, other arithmetic, per_device(): leading = jnp.linalg.cholesky(natural_rows(top_panel))  173 us
    another operation x3, other arithmetic, per_device(): lax.linalg.triangular_solve(leading, row_panel, left_side=False, lower=Tr...  84.6 us
    all_gather x1, waiting for transfers between devices, per_device(): lax.all_gather(own_x, ('prow', 'pcol'), axis=1, tiled=True)  80.7 us
    all_gather x1, waiting for transfers between devices, per_device(): lax.all_gather(own_z, ('prow', 'pcol'), axis=1, tiled=True)  68.9 us
    all_gather x1, waiting for transfers between devices, per_device(): row_panel = lax.all_gather(front_cols, 'pcol', axis=1, tiled=True)  44.1 us
    another operation x24, local copies, waits for them, and re-layouts  28 us
    all_gather x1, waiting for transfers between devices, per_device(): lax.all_gather(row_panel[:lead_rows], 'prow', axis=0, tiled=True)  27.4 us
    all_gather x1, waiting for transfers between devices, per_device(): lax.all_gather(schur_local[:lead_rows], 'prow', axis=0, tiled=True)  24.3 us
  transfers between devices with their start and end apart: 6, of which 5 were waited for; matrix products, arithmetic and copies ran while one was open for 7% of the time, Pallas kernels for 0%

commit v1 on v0

--- a/solution.py
+++ b/solution.py
@@ -1,3 +1,4 @@
+import functools
 import jax
 import jax.numpy as jnp
 from jax import lax
@@ -7,6 +8,18 @@
 NB = 64
 K = 1024
 rank_signs = (1.0, 1.0, -1.0, -1.0)
+
+
+def _store_field(here_x, d0):
+    return jnp.concatenate(
+        lax.all_to_all(
+            jnp.stack([here_x] * lax.axis_size(("prow", "pcol")), 0), ("prow", "pcol"), 0, 0
+        ),
+        d0,
+    )
+
+
+group_ends = functools.partial(_store_field, d0=1)
 
 
 def project(segment, factor_mat):
@@ -63,7 +76,7 @@
             own_x,
             own_z,
             lax.all_gather(own_x, ("prow", "pcol"), axis=1, tiled=True),
-            lax.all_gather(own_z, ("prow", "pcol"), axis=1, tiled=True),
+            group_ends(own_z),
         )
     )
     device_id = lax.axis_index(("prow", "pcol"))

time: 754 us -> 895 us (1.19)
  waiting for transfers between devices: 245 us -> 356 us
  local copies, waits for them, and re-layouts: 106 us -> 126 us
  starting transfers between devices: 7.58 us -> 20.6 us
    all_to_all x0 -> x1, waiting for transfers between devices: none -> 260 us  [_store_field(): lax.all_to_all(jnp.stack([here_x] * lax.axis_size(('prow', 'pcol')), 0),...]
    all_gather x1, waiting for transfers between devices: 80.7 us -> 0.01 us  [per_device(): lax.all_gather(own_x, ('prow', 'pcol'), axis=1, tiled=True)]
    all_gather x1 -> x0, waiting for transfers between devices: 68.9 us -> none  [per_device(): lax.all_gather(own_z, ('prow', 'pcol'), axis=1, tiled=True)]
    all_to_all x0 -> x1, local copies, waits for them, and re-layouts: none -> 14.1 us  [_store_field(): lax.all_to_all(jnp.stack([here_x] * lax.axis_size(('prow', 'pcol')), 0),...]
    all_to_all x0 -> x1, starting transfers between devices: none -> 11.9 us  [_store_field(): lax.all_to_all(jnp.stack([here_x] * lax.axis_size(('prow', 'pcol')), 0),...]
    another operation x24 -> x25, local copies, waits for them, and re-layouts: 28 us -> 34 us
  transfers between devices with their start and end apart: 6 -> 6, of which waited for: 5 -> 4; matrix products, arithmetic and copies ran while one was open for 7% -> 6% of each run, Pallas kernels for 0% -> 0%
where the time goes in v1:
time: 895 us; the launch traced here: 885 us
  waiting for transfers between devices  356 us (40%)
  other arithmetic  269 us (30%)
  local copies, waits for them, and re-layouts  126 us (14%)
  matrix products  92.8 us (10%)
  starting transfers between devices  20.6 us (2%)
  between operations  19.9 us (2%)
    all_to_all x1, waiting for transfers between devices, _store_field(): lax.all_to_all(jnp.stack([here_x] * lax.axis_size(('prow', 'pcol')), 0),...  260 us
    another operation x31, other arithmetic, per_device(): leading = jnp.linalg.cholesky(natural_rows(top_panel))  173 us
    another operation x3, other arithmetic, per_device(): lax.linalg.triangular_solve(leading, row_panel, left_side=False, lower=Tr...  84.6 us
    all_gather x1, waiting for transfers between devices, per_device(): row_panel = lax.all_gather(front_cols, 'pcol', axis=1, tiled=True)  44 us
    another operation x24, local copies, waits for them, and re-layouts  28 us
    all_gather x1, waiting for transfers between devices, per_device(): lax.all_gather(row_panel[:lead_rows], 'prow', axis=0, tiled=True)  27.4 us
    all_gather x1, waiting for transfers between devices, per_device(): lax.all_gather(schur_local[:lead_rows], 'prow', axis=0, tiled=True)  24.4 us
    another operation x14, matrix products, per_device(): leading = jnp.linalg.cholesky(natural_rows(top_panel))  23.1 us
  transfers between devices with their start and end apart: 6, of which 4 were waited for; matrix products, arithmetic and copies ran while one was open for 6% of the time, Pallas kernels for 0%

profile of v1, /device:TPU:1, one launch (start us, length us, event | category | flops | bytes accessed | tf_op | source)
XLA Modules:
  0.0 884.6 jit_solution(13920689809044193173)
XLA Ops:
  11.4 6.0 stack.3
  17.4 11.9 %all-to-all-start = ((bf16[128,4,32,512]{3,2,1,0:T(8,128)(2,1)}), bf16[128,4,32,512]{3,2,1,0:T(8,128)(2,1)}, u32[]{:S(2)}, u32[]{:S(2)}) async-start(bf16[128,4,32,512]{3,2,1,0:T(8,128)(2,1)} %stack.3), calls=%async_computation | async-start | bytes 33554432 | tf_op jit(solution)/shard_map/all_to_all | solution.py:15
  30.0 259.7 %all-to-all-done = bf16[128,4,32,512]{3,2,1,0:T(8,128)(2,1)} async-done(((bf16[128,4,32,512]{3,2,1,0:T(8,128)(2,1)}), bf16[128,4,32,512]{3,2,1,0:T(8,128)(2,1)}, u32[]{:S(2)}, u32[]{:S(2)}) %all-to-all-start) | async-done | bytes 16777248 | tf_op jit(solution)/shard_map/all_to_all | solution.py:15
  289.7 14.1 %copy.45 = bf16[128,4,32,512]{3,2,0,1:T(8,128)(2,1)} copy(bf16[128,4,32,512]{3,2,1,0:T(8,128)(2,1)} %all-to-all-done) | data formatting | bytes 33554432 | tf_op jit(solution)/shard_map/all_to_all | solution.py:15
  303.8 14.5 %fusion.113 = f32[128,16384]{1,0:T(8,128)} fusion(bf16[128,512]{1,0:T(8,128)(2,1)S(1)} %copy-done.4, bf16[16384,512]{1,0:T(8,128)(2,1)} %bitcast.191), kind=kOutput, calls=%fused_computation.289 | convolution fusion | flops 2147483648 | bytes 25296896 | tf_op jit(solution)/shard_map/dot_general | solution.py:38
  318.3 12.9 %convolution_multiply_fusion = f32[128,16384]{1,0:T(8,128)} fusion(f32[128,16384]{1,0:T(8,128)} %fusion.113, bf16[128,512]{1,0:T(8,128)(2,1)S(1)} %convolution_convert_fusion, bf16[16384,512]{1,0:T(8,128)(2,1)} %bitcast.188), kind=kOutput, calls=%fused_computation.7 | convolution fusion | flops 2149580800 | bytes 33685504 | tf_op jit(solution)/shard_map/dot_general | solution.py:44
  331.2 10.8 %reshape.349 = f32[4,32,4,4096]{3,2,1,0:T(4,128)} reshape(f32[128,16384]{1,0:T(8,128)} %convolution_multiply_fusion) | data formatting | bytes 16777216 | tf_op jit(solution)/shard_map/reshape | solution.py:50
  342.0 6.4 multiply_reduce_fusion
  349.1 12.5 %scatter_custom_fusion = f32[32,4096]{0,1:T(8,128)} fusion(s32[4096]{0:T(1024)S(1)} %get-tuple-element.100, f32[32,4096]{0,1:T(8,128)S(1)} %copy.69, f32[]{:T(128)} %constant.382.clone.1), kind=kCustom, calls=%fused_computation.13 | custom fusion | bytes 2621444 | tf_op jit(solution)/shard_map/scatter | solution.py:74
  361.6 4.7 convolution_bitcast_fusion
  369.9 8.5 all-to-all-start.1
  378.4 15.5 %scatter_custom_fusion.1 = s32[4096]{0:T(1024)S(1)} fusion(s32[4096]{0:T(1024)S(1)} %get-tuple-element.100, s32[4096]{0:T(1024)S(1)} %iota.176, s32[]{:T(128)} %copy.148), kind=kCustom, calls=%fused_computation.235 | custom fusion | bytes 16388 | tf_op jit(solution)/shard_map/scatter | solution.py:67
  394.5 3.1 gather_fusion
  397.7 3.1 gather_fusion.1
  404.1 44.0 %all-gather.7.cloned.1.call-done = f32[512,1024]{0,1:T(8,128)} async-done(((f32[512,64]{0,1:T(8,128)}), f32[512,1024]{0,1:T(8,128)}) %all-gather.7.cloned.1.call-update) | async-done | bytes 2097168 | tf_op jit(solution)/shard_map/all_gather | solution.py:116
  450.3 24.4 %all-gather.11.cloned.1.call-done = f32[1024,256]{1,0:T(8,128)} async-done(((f32[128,256]{1,0:T(8,128)}), f32[1024,256]{1,0:T(8,128)}) %all-gather.11.cloned.1.call-update) | async-done | bytes 1048592 | tf_op jit(solution)/shard_map/all_gather | solution.py:125
  481.7 27.4 %all-gather.9.cloned.1.call-done = f32[1024,1024]{1,0:T(8,128)} async-done(((f32[128,1024]{1,0:T(8,128)}), f32[1024,1024]{1,0:T(8,128)}) %all-gather.9.cloned.1.call-update) | async-done | bytes 4194320 | tf_op jit(solution)/shard_map/all_gather | solution.py:124
  509.1 4.7 copy.53
  513.8 5.5 copy.54
  519.3 4.4 fusion
  525.7 11.7 %cholesky.223 = f32[128,128]{1,0:T(8,128)S(1)} custom-call(f32[128,128]{1,0:T(8,128)S(1)} %cholesky.580), custom_call_target="Cholesky" | custom-call | tf_op jit(solution)/shard_map/jit(cholesky)/cholesky | solution.py:135
  539.9 9.8 %custom-call.64 = f32[1,128,128]{1,2,0:T(8,128)S(1)} custom-call(f32[1,128,128]{2,1,0:T(8,128)S(1)} %get-tuple-element.98), custom_call_target="InvertDiagBlocksLowerTriangular" | custom-call | tf_op jit(solution)/shard_map/jit(cholesky)/cholesky | solution.py:135
  553.7 11.9 %cholesky.244 = f32[128,128]{1,0:T(8,128)S(1)} custom-call(f32[128,128]{1,0:T(8,128)S(1)} %cholesky.584), custom_call_target="Cholesky" | custom-call | tf_op jit(solution)/shard_map/jit(cholesky)/cholesky | solution.py:135
  567.5 9.8 %custom-call.65 = f32[1,128,128]{1,2,0:T(8,128)S(1)} custom-call(f32[1,128,128]{2,1,0:T(8,128)S(1)} %get-tuple-element.95), custom_call_target="InvertDiagBlocksLowerTriangular" | custom-call | tf_op jit(solution)/shard_map/jit(cholesky)/cholesky | solution.py:135
  580.7 11.7 %cholesky.468 = f32[128,128]{1,0:T(8,128)S(1)} custom-call(f32[128,128]{1,0:T(8,128)S(1)} %cholesky.589), custom_call_target="Cholesky" | custom-call | tf_op jit(solution)/shard_map/jit(cholesky)/cholesky | solution.py:135
  593.7 9.8 %custom-call.66 = f32[1,128,128]{1,2,0:T(8,128)S(1)} custom-call(f32[1,128,128]{2,1,0:T(8,128)S(1)} %get-tuple-element.92), custom_call_target="InvertDiagBlocksLowerTriangular" | custom-call | tf_op jit(solution)/shard_map/jit(cholesky)/cholesky | solution.py:135
  607.1 12.1 %cholesky.487 = f32[128,128]{1,0:T(8,128)S(1)} custom-call(f32[128,128]{1,0:T(8,128)S(1)} %cholesky.594), custom_call_target="Cholesky" | custom-call | tf_op jit(solution)/shard_map/jit(cholesky)/cholesky | solution.py:135
  620.5 9.8 %custom-call.67 = f32[1,128,128]{1,2,0:T(8,128)S(1)} custom-call(f32[1,128,128]{2,1,0:T(8,128)S(1)} %get-tuple-element.89), custom_call_target="InvertDiagBlocksLowerTriangular" | custom-call | tf_op jit(solution)/shard_map/jit(cholesky)/cholesky | solution.py:135
  633.8 11.7 %cholesky.506 = f32[128,128]{1,0:T(8,128)S(1)} custom-call(f32[128,128]{1,0:T(8,128)S(1)} %cholesky.599), custom_call_target="Cholesky" | custom-call | tf_op jit(solution)/shard_map/jit(cholesky)/cholesky | solution.py:135
  646.8 9.9 %custom-call.68 = f32[1,128,128]{1,2,0:T(8,128)S(1)} custom-call(f32[1,128,128]{2,1,0:T(8,128)S(1)} %get-tuple-element.86), custom_call_target="InvertDiagBlocksLowerTriangular" | custom-call | tf_op jit(solution)/shard_map/jit(cholesky)/cholesky | solution.py:135
  660.1 11.7 %cholesky.526 = f32[128,128]{1,0:T(8,128)S(1)} custom-call(f32[128,128]{1,0:T(8,128)S(1)} %cholesky.604), custom_call_target="Cholesky" | custom-call | tf_op jit(solution)/shard_map/jit(cholesky)/cholesky | solution.py:135
  673.1 9.8 %custom-call.69 = f32[1,128,128]{1,2,0:T(8,128)S(1)} custom-call(f32[1,128,128]{2,1,0:T(8,128)S(1)} %get-tuple-element.83), custom_call_target="InvertDiagBlocksLowerTriangular" | custom-call | tf_op jit(solution)/shard_map/jit(cholesky)/cholesky | solution.py:135
  685.9 11.9 %cholesky.546 = f32[128,128]{1,0:T(8,128)S(1)} custom-call(f32[128,128]{1,0:T(8,128)S(1)} %cholesky.609), custom_call_target="Cholesky" | custom-call | tf_op jit(solution)/shard_map/jit(cholesky)/cholesky | solution.py:135
  699.1 9.8 %custom-call.70 = f32[1,128,128]{1,2,0:T(8,128)S(1)} custom-call(f32[1,128,128]{2,1,0:T(8,128)S(1)} %get-tuple-element.80), custom_call_target="InvertDiagBlocksLowerTriangular" | custom-call | tf_op jit(solution)/shard_map/jit(cholesky)/cholesky | solution.py:135
  711.5 11.7 %cholesky.564 = f32[128,128]{1,0:T(8,128)S(1)} custom-call(f32[128,128]{1,0:T(8,128)S(1)} %convolution_subtract_fusion.21), custom_call_target="Cholesky" | custom-call | tf_op jit(solution)/shard_map/jit(cholesky)/cholesky | solution.py:135
  729.8 4.8 select_select_fusion
  734.6 28.0 %while.1 = (s32[]{:T(128)}, f32[1024,1024]{1,0:T(8,128)}, s32[8,2]{0,1:T(2,128)S(1)}, f32[8,128,128]{2,1,0:T(8,128)}, s32[]{:T(128)}) while((s32[]{:T(128)}, f32[1024,1024]{1,0:T(8,128)}, s32[8,2]{0,1:T(2,128)S(1)}, f32[8,128,128]{2,1,0:T(8,128)}, s32[]{:T(128)}) %tuple.90), condition=%wide.while_cond, body=%wide.while_body.sunk | while | flops 2 | bytes 132705 | solution.py:136
  735.2 2.9 bitcast_dynamic-update-slice_fusion.2
  738.7 2.9 bitcast_dynamic-update-slice_fusion.2
  742.2 2.9 bitcast_dynamic-update-slice_fusion.2
  745.7 2.9 bitcast_dynamic-update-slice_fusion.2
  749.2 2.9 bitcast_dynamic-update-slice_fusion.2
  752.7 2.9 bitcast_dynamic-update-slice_fusion.2
  756.2 2.9 bitcast_dynamic-update-slice_fusion.2
  759.7 2.8 bitcast_dynamic-update-slice_fusion.2
  762.6 79.8 %custom-call.71 = f32[8,128,128]{1,2,0:T(8,128)S(1)} custom-call(f32[8,128,128]{2,1,0:T(8,128)} %get-tuple-element.9), custom_call_target="InvertDiagBlocksLowerTriangular" | custom-call | tf_op jit(solution)/shard_map/triangular_solve | solution.py:136
  869.2 3.1 convolution_subtract_fusion.4
  872.7 4.4 convolution_subtract_fusion
  (161 shorter events, 91.6 us)
Async XLA Ops:
  7.2 1.1 copy-start
  7.2 296.7 %all-gather.5.cloned.1.call-start = ((), (), s32[]{:S(2)}) async-start(), calls=%async_computation.2 | async-start | bytes 16908288 | tf_op jit(solution)/shard_map/all_gather | solution.py:78
  17.4 12.0 %copy-start.9 = (s32[4096]{0:T(1024)S(1)}, s32[4096]{0:T(1024)}, u32[]{:S(2)}) copy-start(s32[4096]{0:T(1024)} %param.8) | copy-start | bytes 49156
  17.4 12.2 %copy-start.10 = (f32[4]{0:T(128)S(1)}, f32[4]{0:T(128)}, u32[]{:S(2)}) copy-start(f32[4]{0:T(128)} %constant.397.clone) | copy-start | bytes 52
  17.4 272.3 %all-to-all-start = ((bf16[128,4,32,512]{3,2,1,0:T(8,128)(2,1)}), bf16[128,4,32,512]{3,2,1,0:T(8,128)(2,1)}, u32[]{:S(2)}, u32[]{:S(2)}) async-start(bf16[128,4,32,512]{3,2,1,0:T(8,128)(2,1)} %stack.3), calls=%async_computation | async-start | bytes 33554432 | tf_op jit(solution)/shard_map/all_to_all | solution.py:15
  30.0 273.8 %copy-start.4 = (bf16[128,512]{1,0:T(8,128)(2,1)S(1)}, bf16[128,512]{1,0:T(8,128)(2,1)}, u32[]{:S(2)}) copy-start(bf16[128,512]{1,0:T(8,128)(2,1)} %convolution_convert_fusion.1) | copy-start | bytes 393220
  369.9 31.1 %all-to-all-start.1 = ((f32[128,8,256]{2,1,0:T(8,128)}), f32[128,8,256]{2,1,0:T(8,128)S(1)}, u32[]{:S(2)}, u32[]{:S(2)}) async-start(f32[128,8,256]{2,1,0:T(8,128)} %reshape_reshape.7), calls=%async_computation.1 | async-start | bytes 2097152 | tf_op jit(solution)/shard_map/all_to_all | solution.py:98
  378.3 69.8 %all-gather.7.cloned.1.call-start = ((), (), s32[]{:S(2)}) async-start(), calls=%async_computation.3 | async-start | bytes 2228224 | tf_op jit(solution)/shard_map/all_gather | solution.py:116
  403.3 71.4 %all-gather.11.cloned.1.call-start = ((), (), s32[]{:S(2)}) async-start(), calls=%async_computation.5 | async-start | bytes 1179648 | tf_op jit(solution)/shard_map/all_gather | solution.py:125
  404.1 105.0 %all-gather.9.cloned.1.call-start = ((), (), s32[]{:S(2)}) async-start(), calls=%async_computation.4 | async-start | bytes 4718592 | tf_op jit(solution)/shard_map/all_gather | solution.py:124
  523.8 1.9 copy-start.3
  842.4 6.0 copy-start.2
  849.4 7.1 copy-start.5
  851.0 6.6 copy-start.6
  856.5 4.7 copy-start.8
  863.0 6.2 copy-start.7
  868.8 9.0 %copy-start.1 = (bf16[512,512]{1,0:T(8,128)(2,1)S(1)}, bf16[512,512]{1,0:T(8,128)(2,1)}, u32[]{:S(2)}) copy-start(bf16[512,512]{1,0:T(8,128)(2,1)} %param.6) | copy-start | bytes 1572868
Sparse Core Ops, SparseCore 0:
  11.6 248.3 all-gather.4
  403.4 44.6 all-gather.6
  449.9 24.7 all-gather.10
  476.8 32.1 all-gather.8
